TPU v7x, 256 devices: a whole 4x4x8 slice. The times are simulated.
256 devices in a mesh: row: 16 (over y, x), col: 16 (over z, core).
Axes of the slice: x: 4, y: 4, z: 8, core: 2. Of those that a mesh axis runs over, the one named last changes fastest.
Arguments:
- features: bfloat16 [512, 512, 128], P('col')
- diag_inverse: bfloat16 [512, 128, 128], P('col')
- precision_tiles: float32 [16, 16, 32, 128, 128], P('row', 'col'), may hold values from -3 to 3
- inverse_tiles: float32 [16, 16, 32, 128, 128], P('row', 'col'), may hold values from -0.3125 to 0.3125
- slot_rows: int32 [16, 16, 32], replicated, may hold values from 0 to 511, as said below
- slot_columns: int32 [16, 16, 32], replicated, may hold values from 0 to 1, as said below
- owned_columns: int32 [16, 16, 2], replicated, may hold values from 0 to 511, as said below
- live_counts: int32 [16, 16], replicated, may hold values from 1 to 32, as said below
Outputs:
- direction: float32 [16, 16, 32, 128, 128], P('row', 'col')
Inputs may be any that keep to these rules, and one draw needn't show every extreme that they name: `slot_rows`: slot k of every owner names a block-row held by index k // 2 of col, that is one of feature blocks 32 * (k // 2) to 32 * (k // 2) + 31; no pair of block-row and block-column is named by two slots of the whole grid. `slot_columns`: some owner uses every entry of its list. `owned_columns`: an owner's 2 block-columns are distinct and lie among the feature blocks of its own index of col. The live slots of an owner are slots 0 to live_counts - 1; some owner has all 32 slots live.
All inputs are finite; a program needn't handle non-finite values.
Results may differ from a plain program's by a relative error of at most 0.0003.
Values may be sent and summed in bfloat16 or wider, within the bound.
No kernel may reach another device: no remote copies, remote signals or barrier semaphores. Data moves between devices by JAX's collectives and lax.ppermute only.
A program may use at most 128 MiB of HBM per device.

v0:
```python
import jax
import jax.numpy as jnp
from jax import lax
from jax.sharding import PartitionSpec as P

SWEEPS = 4
step_size = 0.3
penalty = 0.6
highest = lax.Precision.HIGHEST


def soft_update(precision_tile, direction, residual):
    shifted = precision_tile + direction - step_size * residual
    return (
        jnp.sign(shifted) * jnp.maximum(jnp.abs(shifted) - step_size * penalty, 0.0)
        - precision_tile
    )


def body(
    features,
    diag_inverse,
    precision_tiles,
    inverse_tiles,
    slot_rows,
    slot_columns,
    owned_columns,
    live_counts,
):
    col_count = lax.axis_size("col")
    row_index = lax.axis_index("row")
    col_index = lax.axis_index("col")
    block_count = features.shape[0]
    sample_count = features.shape[1]
    block_size = features.shape[2]
    slot_count = precision_tiles.shape[2]
    per_source = slot_count // col_count
    row_table = slot_rows[row_index]
    wanted = jnp.take(row_table.reshape(col_count, col_count, per_source), col_index, axis=1)
    local_rows = (wanted - col_index * block_count).reshape(-1)
    send_tiles = jnp.take(features, local_rows, axis=0).reshape(
        col_count, per_source, sample_count, block_size
    )
    send_diag = jnp.take(diag_inverse, local_rows, axis=0).reshape(
        col_count, per_source, block_size, block_size
    )
    row_tiles, row_diag = (
        lax.all_to_all(send_tiles, "col", split_axis=0, concat_axis=0, tiled=True),
        lax.all_to_all(send_diag, "col", split_axis=0, concat_axis=0, tiled=True),
    )
    row_tiles = row_tiles.reshape(slot_count, sample_count, block_size)
    row_diag = row_diag.reshape(slot_count, block_size, block_size).astype(jnp.float32)
    my_lists = slot_columns[row_index, col_index]
    my_owned = owned_columns[row_index, col_index]
    column_ids = jnp.take(my_owned, my_lists)
    local_cols = column_ids - col_index * block_count
    live_mask = (jnp.arange(slot_count) < live_counts[row_index, col_index]).astype(jnp.float32)
    col_tiles = jnp.take(features, local_cols, axis=0)
    covariance = (
        jnp.einsum("kna,knb->kab", row_tiles, col_tiles, preferred_element_type=jnp.float32)
        / sample_count
    )
    tiles_here = inverse_tiles[0, 0]
    theta_here = precision_tiles[0, 0]
    gradient = covariance - tiles_here
    col_diag = jnp.take(diag_inverse, local_cols, axis=0).astype(jnp.float32)
    direction = jnp.zeros_like(gradient)
    for sweep_index in range(SWEEPS):
        residual = gradient
        if sweep_index > 0:
            left_side = jnp.einsum("kab,kbc->kac", row_diag, direction, precision=highest)
            residual = residual + jnp.einsum("kac,kcd->kad", left_side, col_diag, precision=highest)
            products = (
                jnp.einsum("kba,kbc->kac", direction, tiles_here, precision=highest)
                * live_mask[:, None, None]
            )
            onehot = (local_cols[:, None] == jnp.arange(block_count)[None, :]).astype(jnp.float32)
            dense_sums = jnp.einsum("kf,kab->fab", onehot, products, precision=highest)
            summed = lax.psum(dense_sums, "row")
            residual = residual + jnp.einsum(
                "kab,kbc->kac",
                tiles_here,
                jnp.einsum("kf,fab->kab", onehot, summed, precision=highest),
                precision=highest,
            )
        direction = soft_update(theta_here, direction, residual)
    return (direction * live_mask[:, None, None]).reshape(precision_tiles.shape)


def solution(mesh):
    return jax.shard_map(
        body,
        mesh=mesh,
        in_specs=(
            P("col", None, None),
            P("col", None, None),
            P("row", "col", None, None, None),
            P("row", "col", None, None, None),
            P(),
            P(),
            P(),
            P(),
        ),
        out_specs=P("row", "col", None, None, None),
        check_vma=False,
    )
```

profile of v0, /device:TPU:1, one launch (start us, length us, event | category | flops | bytes accessed | tf_op | source)
XLA Modules:
  0.0 511.0 jit_solution(2454693895170861494)
XLA Ops:
  6.5 0.0 copy-start
  6.5 0.8 constant_dynamic-slice_fusion
  7.4 0.5 fusion.89
  7.9 0.7 constant_dynamic-slice_fusion.2
  8.6 0.1 copy.34
  8.7 0.1 copy.14
  8.8 0.1 sub.61
  8.9 2.0 compare_and_fusion
  10.9 5.2 %gather_fusion = bf16[32,512,128]{2,1,0:T(8,128)(2,1)} fusion(bf16[32,512,128]{2,1,0:T(8,128)(2,1)} %param.12, s32[1024]{0:T(1024)S(1)} %pad_clamp_fusion.1), kind=kCustom, calls=%fused_computation.clone | custom fusion | bytes 8388736 | tf_op jit(solution)/shard_map/jit(_take)/gather | solution.py:41
  16.1 4.6 broadcast_select_fusion
  20.7 6.5 %copy.15 = bf16[16,2,512,128]{2,3,1,0:T(8,128)(2,1)} copy(bf16[16,2,512,128]{3,2,1,0:T(8,128)(2,1)} %bitcast.129) | data formatting | bytes 8388608 | tf_op jit(solution)/shard_map/reshape | solution.py:41
  27.2 10.0 %all-to-all-start = ((bf16[16,2,512,128]{2,3,1,0:T(8,128)(2,1)}), bf16[16,2,512,128]{2,3,1,0:T(8,128)(2,1)}, u32[]{:S(2)}, u32[]{:S(2)}) async-start(bf16[16,2,512,128]{2,3,1,0:T(8,128)(2,1)} %copy.15), calls=%async_computation | async-start | bytes 8388608 | tf_op jit(solution)/shard_map/all_to_all | solution.py:48
  37.1 1.3 dynamic_slice.15
  38.4 0.0 copy-done
  38.4 1.6 gather_fusion.2
  40.1 5.2 %gather_fusion.1 = bf16[32,512,128]{2,1,0:T(8,128)(2,1)} fusion(bf16[32,512,128]{2,1,0:T(8,128)(2,1)} %param.12, s32[1024]{0:T(1024)S(1)} %pad_clamp_fusion), kind=kCustom, calls=%fused_computation.2.clone | custom fusion | bytes 8388736 | tf_op jit(solution)/shard_map/jit(_take)/gather | solution.py:58
  45.3 0.6 compare_convert_fusion
  45.9 0.0 copy-start.2
  45.9 2.5 broadcast_select_fusion.2
  48.5 82.3 %all-to-all-done = bf16[16,2,512,128]{2,3,1,0:T(8,128)(2,1)} async-done(((bf16[16,2,512,128]{2,3,1,0:T(8,128)(2,1)}), bf16[16,2,512,128]{2,3,1,0:T(8,128)(2,1)}, u32[]{:S(2)}, u32[]{:S(2)}) %all-to-all-start) | async-done | bytes 4194336 | tf_op jit(solution)/shard_map/all_to_all | solution.py:48
  130.7 5.5 %all-to-all-start.1 = ((bf16[16,2,128,128]{3,2,1,0:T(8,128)(2,1)}), bf16[16,2,128,128]{3,2,1,0:T(8,128)(2,1)}, u32[]{:S(2)}, u32[]{:S(2)}) async-start(bf16[16,2,128,128]{3,2,1,0:T(8,128)(2,1)} %bitcast.130), calls=%async_computation.1 | async-start | bytes 2097152 | tf_op jit(solution)/shard_map/all_to_all | solution.py:49
  136.3 0.2 all-reduce.4.cloned.1.call-start
  136.5 0.0 copy-done.2
  136.5 0.0 copy-start.3
  136.5 4.9 bitcast_subtract_fusion
  141.4 0.0 copy-done.3
  141.4 0.0 copy-start.7
  141.5 4.5 fusion.39
  146.0 0.0 copy-done.7
  146.0 2.5 fusion.36
  148.5 2.5 copy.20
  151.0 0.0 all-reduce.4.cloned.1.call-update
  151.0 0.3 all-reduce.6.cloned.1.call-start
  151.3 1.7 gather_fusion.3
  153.0 11.3 %all-to-all-done.1 = bf16[16,2,128,128]{3,2,1,0:T(8,128)(2,1)} async-done(((bf16[16,2,128,128]{3,2,1,0:T(8,128)(2,1)}), bf16[16,2,128,128]{3,2,1,0:T(8,128)(2,1)}, u32[]{:S(2)}, u32[]{:S(2)}) %all-to-all-start.1) | async-done | bytes 1048608 | tf_op jit(solution)/shard_map/all_to_all | solution.py:49
  164.3 4.8 fusion.62
  169.1 0.0 copy-done.13
  169.1 2.6 fusion.87
  171.7 79.8 %all-reduce.4.cloned.1.call-done = f32[32,128,128]{2,1,0:T(8,128)} async-done(((f32[32,128,128]{2,1,0:T(8,128)}), f32[32,128,128]{2,1,0:T(8,128)}) %all-reduce.4.cloned.1.call-update) | async-done | bytes 2097168 | tf_op jit(solution)/shard_map/psum | solution.py:79
  251.5 4.1 fusion.34
  255.6 0.0 copy-done.4
  255.6 0.0 copy-done.8
  255.6 6.9 %bitcast_subtract_fusion.3 = f32[32,128,128]{2,1,0:T(8,128)S(1)} fusion(f32[1,1,32,128,128]{4,3,2,1,0:T(8,128)S(1)} %copy-done.4, f32[32,128,128]{2,1,0:T(8,128)S(1)} %copy-done.8, f32[32,128,128]{2,1,0:T(8,128)} %fusion.87, f32[1,1,32,128,128]{4,3,2,1,0:T(8,128)S(1)} %copy-done.2, f32[32,128,128]{2,0,1:T(8,128)S(1)} %fusion.34), kind=kOutput, calls=%fused_computation.34 | convolution fusion | flops 815267840 | bytes 12582912 | tf_op jit(solution)/shard_map/kab,kbc->kac/dot_general | solution.py:80
  262.5 4.3 fusion.42
  266.8 2.5 fusion.31
  269.3 2.6 copy.25
  271.9 0.0 all-reduce.6.cloned.1.call-update
  271.9 0.0 all-reduce.8.cloned.1.call-start
  272.0 3.2 fusion.90
  275.1 2.5 fusion.86
  277.7 94.3 %all-reduce.6.cloned.1.call-done = f32[32,128,128]{2,1,0:T(8,128)} async-done(((f32[32,128,128]{2,1,0:T(8,128)}), f32[32,128,128]{2,1,0:T(8,128)}) %all-reduce.6.cloned.1.call-update) | async-done | bytes 2097168 | tf_op jit(solution)/shard_map/psum | solution.py:79
  371.9 4.1 fusion.29
  376.0 6.9 %bitcast_subtract_fusion.2 = f32[32,128,128]{2,1,0:T(8,128)S(1)} fusion(f32[1,1,32,128,128]{4,3,2,1,0:T(8,128)S(1)} %copy-done.5, f32[32,128,128]{2,1,0:T(8,128)} %copy-done.12, f32[32,128,128]{2,1,0:T(8,128)S(1)} %copy-done.9, f32[32,128,128]{2,1,0:T(8,128)} %fusion.86, f32[1,1,32,128,128]{4,3,2,1,0:T(8,128)S(1)} %copy-done.2, f32[32,128,128]{2,0,1:T(8,128)S(1)} %fusion.29), kind=kOutput, calls=%fused_computation.32 | convolution fusion | flops 811073536 | bytes 14680064 | tf_op jit(solution)/shard_map/kab,kbc->kac/dot_general | solution.py:80
  383.0 0.0 copy-start.11
  383.0 4.0 fusion.45
  387.0 2.5 fusion.26
  389.5 2.6 copy.30
  392.1 0.0 all-reduce.8.cloned.1.call-update
  392.1 3.2 fusion.91
  395.3 2.6 fusion.85
  397.8 94.2 %all-reduce.8.cloned.1.call-done = f32[32,128,128]{2,1,0:T(8,128)} async-done(((f32[32,128,128]{2,1,0:T(8,128)}), f32[32,128,128]{2,1,0:T(8,128)}) %all-reduce.8.cloned.1.call-update) | async-done | bytes 2097168 | tf_op jit(solution)/shard_map/psum | solution.py:79
  492.0 4.3 fusion.24
  496.4 0.0 copy-start.1
  496.4 7.9 %fusion.22 = f32[1,1,32,128,128]{4,3,2,1,0:T(8,128)} fusion(f32[1,1,32,128,128]{4,3,2,1,0:T(8,128)S(1)} %copy-done.6, f32[32,128,128]{2,1,0:T(8,128)} %copy-done.11, f32[32,128,128]{2,1,0:T(8,128)S(1)} %copy-done.10, f32[32,128,128]{2,1,0:T(8,128)} %fusion.85, f32[1,1,32,128,128]{4,3,2,1,0:T(8,128)S(1)} %copy-done.2, f32[32,128,128]{2,0,1:T(8,128)S(1)} %fusion.24, ...), kind=kOutput, calls=%fused_computation.39 | convolution fusion | flops 811597824 | bytes 14680192 | tf_op jit(solution)/shard_map/kab,kbc->kac/dot_general | solution.py:80
  (20 shorter events, 0.1 us)
Async XLA Ops:
  6.5 31.9 %copy-start = (bf16[32,128,128]{2,1,0:T(8,128)(2,1)S(1)}, bf16[32,128,128]{2,1,0:T(8,128)(2,1)}, u32[]{:S(2)}) copy-start(bf16[32,128,128]{2,1,0:T(8,128)(2,1)} %param.13) | copy-start | bytes 3145732
  27.2 103.6 %all-to-all-start = ((bf16[16,2,512,128]{2,3,1,0:T(8,128)(2,1)}), bf16[16,2,512,128]{2,3,1,0:T(8,128)(2,1)}, u32[]{:S(2)}, u32[]{:S(2)}) async-start(bf16[16,2,512,128]{2,3,1,0:T(8,128)(2,1)} %copy.15), calls=%async_computation | async-start | bytes 8388608 | tf_op jit(solution)/shard_map/all_to_all | solution.py:48
  45.9 90.6 %copy-start.2 = (f32[1,1,32,128,128]{4,3,2,1,0:T(8,128)S(1)}, f32[1,1,32,128,128]{4,3,2,1,0:T(8,128)}, u32[]{:S(2)}) copy-start(f32[1,1,32,128,128]{4,3,2,1,0:T(8,128)} %param.15) | copy-start | bytes 6291460
  130.7 33.6 %all-to-all-start.1 = ((bf16[16,2,128,128]{3,2,1,0:T(8,128)(2,1)}), bf16[16,2,128,128]{3,2,1,0:T(8,128)(2,1)}, u32[]{:S(2)}, u32[]{:S(2)}) async-start(bf16[16,2,128,128]{3,2,1,0:T(8,128)(2,1)} %bitcast.130), calls=%async_computation.1 | async-start | bytes 2097152 | tf_op jit(solution)/shard_map/all_to_all | solution.py:49
  136.3 115.2 %all-reduce.4.cloned.1.call-start = ((), (), s32[]{:S(2)}) async-start(), calls=%async_computation.2 | async-start | bytes 4194304 | tf_op jit(solution)/shard_map/psum | solution.py:79
  136.5 4.9 copy-start.3
  141.4 4.5 copy-start.7
  151.0 220.9 %all-reduce.6.cloned.1.call-start = ((), (), s32[]{:S(2)}) async-start(), calls=%async_computation.3 | async-start | bytes 4194304 | tf_op jit(solution)/shard_map/psum | solution.py:79
  164.3 4.8 copy-start.13
  251.5 4.1 copy-start.4
  251.5 4.1 copy-start.8
  262.5 4.3 copy-start.12
  271.9 220.1 %all-reduce.8.cloned.1.call-start = ((), (), s32[]{:S(2)}) async-start(), calls=%async_computation.4 | async-start | bytes 4194304 | tf_op jit(solution)/shard_map/psum | solution.py:79
  371.9 4.1 copy-start.5
  371.9 4.1 copy-start.9
  383.0 4.0 copy-start.11
  492.0 4.3 copy-start.6
  492.0 4.3 copy-start.10
  496.4 7.9 %copy-start.1 = (bf16[32,128,128]{2,1,0:T(8,128)(2,1)S(1)}, bf16[32,128,128]{2,1,0:T(8,128)(2,1)}, u32[]{:S(2)}) copy-start(bf16[32,128,128]{2,1,0:T(8,128)(2,1)} %param.13) | copy-start | bytes 3145732
Sparse Core Ops, SparseCore 0:
  151.2 100.2 all-reduce.3
  272.0 99.8 all-reduce.5
  392.2 99.7 all-reduce.7
where the time goes:
time: 514 us; the launch traced here: 511 us
  waiting for transfers between devices  362 us (70%)
  matrix products  78.1 us (15%)
  local copies, waits for them, and re-layouts  31.6 us (6%)
  starting transfers between devices  16 us (3%)
  between operations  13.6 us (3%)
  other arithmetic  9.75 us (2%)
    psum x3, waiting for transfers between devices, body(): summed = lax.psum(dense_sums, 'row')  268 us
    all_to_all x1, waiting for transfers between devices, body(): lax.all_to_all(send_tiles, 'col', split_axis=0, concat_axis=0, tiled=True)  82.3 us
    dot_general x3, matrix products, body(): jnp.einsum('kab,kbc->kac', tiles_here, jnp.einsum('kf,fab->kab', onehot,...  21.7 us
    dot_general x3, matrix products, body(): jnp.einsum('kba,kbc->kac', direction, tiles_here, precision=highest)  12.8 us
    dot_general x3, matrix products, body(): jnp.einsum('kf,fab->kab', onehot, summed, precision=highest)  12.4 us
    all_to_all x1, waiting for transfers between devices, body(): lax.all_to_all(send_diag, 'col', split_axis=0, concat_axis=0, tiled=True)  11.3 us
    dot_general x3, matrix products, body(): jnp.einsum('kab,kbc->kac', row_diag, direction, precision=highest)  11.1 us
  transfers between devices with their start and end apart: 5, of which 5 were waited for; matrix products, arithmetic and copies ran while one was open for 9% of the time, Pallas kernels for 0%

commit v1 on v0

--- a/solution.py
+++ b/solution.py
@@ -76,7 +76,8 @@
             )
             onehot = (local_cols[:, None] == jnp.arange(block_count)[None, :]).astype(jnp.float32)
             dense_sums = jnp.einsum("kf,kab->fab", onehot, products, precision=highest)
-            summed = lax.psum(dense_sums, "row")
+            parts = lax.all_gather(dense_sums, "row")
+            summed = jnp.sum(parts, axis=0)
             residual = residual + jnp.einsum(
                 "kab,kbc->kac",
                 tiles_here,

time: 514 us -> 855 us (1.66)
  waiting for transfers between devices: 362 us -> 650 us
  other arithmetic: 9.75 us -> 52.6 us
  starting transfers between devices: 16 us -> 27.2 us
    all_gather x0 -> x3, waiting for transfers between devices: none -> 549 us  [body(): parts = lax.all_gather(dense_sums, 'row')]
    psum x3 -> x0, waiting for transfers between devices: 268 us -> none  [body(): summed = lax.psum(dense_sums, 'row')]
    reduce_sum x0 -> x3, other arithmetic: none -> 42.9 us  [body(): summed = jnp.sum(parts, axis=0)]
    all_gather x0 -> x3, starting transfers between devices: none -> 11.7 us  [body(): parts = lax.all_gather(dense_sums, 'row')]
  transfers between devices with their start and end apart: 5 -> 5, of which waited for: 5 -> 5; matrix products, arithmetic and copies ran while one was open for 9% -> 4% of each run, Pallas kernels for 0% -> 0%
where the time goes in v1:
time: 855 us; the launch traced here: 846 us
  waiting for transfers between devices  650 us (76%)
  matrix products  78.4 us (9%)
  other arithmetic  52.6 us (6%)
  starting transfers between devices  27.2 us (3%)
  local copies, waits for them, and re-layouts  24.1 us (3%)
  between operations  13.6 us (2%)
    all_gather x3, waiting for transfers between devices, body(): parts = lax.all_gather(dense_sums, 'row')  549 us
    all_to_all x1, waiting for transfers between devices, body(): lax.all_to_all(send_tiles, 'col', split_axis=0, concat_axis=0, tiled=True)  86.2 us
    reduce_sum x3, other arithmetic, body(): summed = jnp.sum(parts, axis=0)  42.9 us
    dot_general x3, matrix products, body(): jnp.einsum('kab,kbc->kac', tiles_here, jnp.einsum('kf,fab->kab', onehot,...  22.1 us
  transfers between devices with their start and end apart: 5, of which 5 were waited for; matrix products, arithmetic and copies ran while one was open for 4% of the time, Pallas kernels for 0%

profile of v1, /device:TPU:1, one launch (start us, length us, event | category | flops | bytes accessed | tf_op | source)
XLA Modules:
  0.0 845.7 jit_solution(18233417532113147031)
XLA Ops:
  6.5 0.0 copy-start
  6.5 0.8 constant_dynamic-slice_fusion
  7.4 0.5 fusion.86
  7.9 0.7 constant_dynamic-slice_fusion.2
  8.6 0.1 copy.55
  8.7 0.1 copy.26
  8.8 0.1 sub.61
  8.9 2.0 compare_and_fusion
  10.9 5.3 gather_fusion
  16.1 4.6 broadcast_select_fusion
  20.8 6.4 copy.27
  27.2 10.0 %all-to-all-start = ((bf16[16,2,512,128]{2,3,1,0:T(8,128)(2,1)}), bf16[16,2,512,128]{2,3,1,0:T(8,128)(2,1)}, u32[]{:S(2)}, u32[]{:S(2)}) async-start(bf16[16,2,512,128]{2,3,1,0:T(8,128)(2,1)} %copy.27), calls=%async_computation | async-start | bytes 8388608 | tf_op jit(solution)/shard_map/all_to_all | solution.py:48
  37.2 0.0 all-gather.7.cloned.1.call-start
  37.2 1.3 dynamic_slice.15
  38.5 5.4 gather_fusion.1
  43.9 0.6 compare_convert_fusion
  44.5 86.2 %all-to-all-done = bf16[16,2,512,128]{2,3,1,0:T(8,128)(2,1)} async-done(((bf16[16,2,512,128]{2,3,1,0:T(8,128)(2,1)}), bf16[16,2,512,128]{2,3,1,0:T(8,128)(2,1)}, u32[]{:S(2)}, u32[]{:S(2)}) %all-to-all-start) | async-done | bytes 4194336 | tf_op jit(solution)/shard_map/all_to_all | solution.py:48
  130.8 0.0 copy-done.2
  130.8 4.9 bitcast_subtract_fusion
  135.7 0.0 copy-done.3
  135.7 0.0 copy-start.7
  135.7 4.5 fusion.33
  140.2 0.0 copy-done.7
  140.2 3.7 fusion.30
  144.0 0.0 all-gather.7.cloned.1.call-update
  144.0 0.0 copy-done
  144.0 1.7 gather_fusion.2
  145.7 2.4 broadcast_select_fusion.2
  148.1 5.5 all-to-all-start.1
  153.7 11.6 %all-gather.9.cloned.1.call-start = ((), (), s32[]{:S(2)}) async-start(), calls=%async_computation.3 | async-start | bytes 35651584 | tf_op jit(solution)/shard_map/all_gather | solution.py:79
  165.3 1.7 gather_fusion.3
  166.9 14.8 %all-to-all-done.1 = bf16[16,2,128,128]{3,2,1,0:T(8,128)(2,1)} async-done(((bf16[16,2,128,128]{3,2,1,0:T(8,128)(2,1)}), bf16[16,2,128,128]{3,2,1,0:T(8,128)(2,1)}, u32[]{:S(2)}, u32[]{:S(2)}) %all-to-all-start.1) | async-done | bytes 1048608 | tf_op jit(solution)/shard_map/all_to_all | solution.py:49
  181.7 4.9 fusion.56
  186.7 0.0 copy-done.13
  186.7 2.6 fusion.84
  189.3 156.3 %all-gather.7.cloned.1.call-done = f32[512,128,128]{2,0,1:T(8,128)} async-done(((f32[32,128,128]{2,0,1:T(8,128)}), f32[512,128,128]{2,0,1:T(8,128)}) %all-gather.7.cloned.1.call-update) | async-done | bytes 33554448 | tf_op jit(solution)/shard_map/all_gather | solution.py:79
  345.6 14.3 %reduce_sum.27 = f32[32,128,128]{2,0,1:T(8,128)} reduce(f32[16,32,128,128]{3,1,0,2:T(8,128)} %bitcast.138, f32[]{:T(128)} %constant.75.clone.1), dimensions={0}, to_apply=%region_0.3 | reduce | flops 7864320 | bytes 35651588 | tf_op jit(solution)/shard_map/reduce_sum | solution.py:80
  359.9 2.8 fusion.65
  362.8 0.0 copy-done.4
  362.8 0.0 copy-done.8
  362.8 6.9 bitcast_subtract_fusion.3
  369.7 0.0 copy-start.12
  369.7 3.8 fusion.36
  373.5 0.0 copy-done.12
  373.5 4.0 fusion.27
  377.5 0.0 all-gather.9.cloned.1.call-update
  377.5 0.0 all-gather.11.cloned.1.call-start
  377.5 3.2 fusion.87
  380.7 2.6 fusion.83
  383.3 196.2 %all-gather.9.cloned.1.call-done = f32[512,128,128]{2,0,1:T(8,128)} async-done(((f32[32,128,128]{2,0,1:T(8,128)}), f32[512,128,128]{2,0,1:T(8,128)}) %all-gather.9.cloned.1.call-update) | async-done | bytes 33554448 | tf_op jit(solution)/shard_map/all_gather | solution.py:79
  579.5 14.3 %reduce_sum.28 = f32[32,128,128]{2,0,1:T(8,128)} reduce(f32[16,32,128,128]{3,1,0,2:T(8,128)} %bitcast.140, f32[]{:T(128)} %constant.75.clone.1), dimensions={0}, to_apply=%region_1.4 | reduce | flops 7864320 | bytes 35651588 | tf_op jit(solution)/shard_map/reduce_sum | solution.py:80
  593.8 2.9 fusion.63
  596.7 7.2 bitcast_subtract_fusion.2
  603.9 0.0 copy-start.11
  603.9 4.0 fusion.39
  607.9 3.7 fusion.24
  611.6 0.0 all-gather.11.cloned.1.call-update
  611.7 3.2 fusion.88
  614.9 2.6 fusion.82
  617.4 196.2 %all-gather.11.cloned.1.call-done = f32[512,128,128]{2,0,1:T(8,128)} async-done(((f32[32,128,128]{2,0,1:T(8,128)}), f32[512,128,128]{2,0,1:T(8,128)}) %all-gather.11.cloned.1.call-update) | async-done | bytes 33554448 | tf_op jit(solution)/shard_map/all_gather | solution.py:79
  813.7 14.3 %reduce_sum.29 = f32[32,128,128]{2,0,1:T(8,128)} reduce(f32[16,32,128,128]{3,1,0,2:T(8,128)} %bitcast.139, f32[]{:T(128)} %constant.75.clone.1), dimensions={0}, to_apply=%region_2.5 | reduce | flops 7864320 | bytes 35651588 | tf_op jit(solution)/shard_map/reduce_sum | solution.py:80
  828.0 2.9 fusion.61
  830.9 0.0 copy-start.1
  830.9 8.0 fusion.22
  (20 shorter events, 0.1 us)
Async XLA Ops:
  6.5 137.5 %copy-start = (bf16[32,128,128]{2,1,0:T(8,128)(2,1)S(1)}, bf16[32,128,128]{2,1,0:T(8,128)(2,1)}, u32[]{:S(2)}) copy-start(bf16[32,128,128]{2,1,0:T(8,128)(2,1)} %param.13) | copy-start | bytes 3145732
  27.2 103.6 %all-to-all-start = ((bf16[16,2,512,128]{2,3,1,0:T(8,128)(2,1)}), bf16[16,2,512,128]{2,3,1,0:T(8,128)(2,1)}, u32[]{:S(2)}, u32[]{:S(2)}) async-start(bf16[16,2,512,128]{2,3,1,0:T(8,128)(2,1)} %copy.27), calls=%async_computation | async-start | bytes 8388608 | tf_op jit(solution)/shard_map/all_to_all | solution.py:48
  37.2 308.4 %all-gather.7.cloned.1.call-start = ((), (), s32[]{:S(2)}) async-start(), calls=%async_computation.2 | async-start | bytes 35651584 | tf_op jit(solution)/shard_map/all_gather | solution.py:79
  38.5 92.3 %copy-start.2 = (f32[1,1,32,128,128]{4,3,2,1,0:T(8,128)S(1)}, f32[1,1,32,128,128]{4,3,2,1,0:T(8,128)}, u32[]{:S(2)}) copy-start(f32[1,1,32,128,128]{4,3,2,1,0:T(8,128)} %param.15) | copy-start | bytes 6291460
  130.8 4.9 copy-start.3
  135.7 4.5 copy-start.7
  148.1 33.6 %all-to-all-start.1 = ((bf16[16,2,128,128]{3,2,1,0:T(8,128)(2,1)}), bf16[16,2,128,128]{3,2,1,0:T(8,128)(2,1)}, u32[]{:S(2)}, u32[]{:S(2)}) async-start(bf16[16,2,128,128]{3,2,1,0:T(8,128)(2,1)} %bitcast.142), calls=%async_computation.1 | async-start | bytes 2097152 | tf_op jit(solution)/shard_map/all_to_all | solution.py:49
  153.7 425.8 %all-gather.9.cloned.1.call-start = ((), (), s32[]{:S(2)}) async-start(), calls=%async_computation.3 | async-start | bytes 35651584 | tf_op jit(solution)/shard_map/all_gather | solution.py:79
  181.7 5.0 copy-start.13
  359.9 2.9 copy-start.4
  359.9 2.9 copy-start.8
  369.7 3.8 copy-start.12
  377.5 436.2 %all-gather.11.cloned.1.call-start = ((), (), s32[]{:S(2)}) async-start(), calls=%async_computation.4 | async-start | bytes 35651584 | tf_op jit(solution)/shard_map/all_gather | solution.py:79
  593.8 2.9 copy-start.5
  593.8 2.9 copy-start.9
  603.9 4.0 copy-start.11
  828.0 2.9 copy-start.6
  828.0 2.9 copy-start.10
  830.9 8.0 copy-start.1
Sparse Core Ops, SparseCore 0:
  144.1 201.4 all-gather.6
  377.6 201.8 all-gather.8
  611.8 201.8 all-gather.10
